TPU v7x, 256 devices: a whole 4x4x8 slice. The times are simulated.
256 devices in a mesh: head: 32 (over y, z), dp: 8 (over x, core).
Axes of the slice: x: 4, y: 4, z: 8, core: 2. Of those that a mesh axis runs over, the one named last changes fastest.
Arguments:
- attn_out: bfloat16 [2048, 8192], P('dp', 'head'), may hold values from -6 to 6
- head_mask: int32 [64], P('head'), may hold values from 0 to 1, as said below
- gate_scale: float32 [64], P('head'), may hold values from 0.25 to 2
- w_out: bfloat16 [8192, 8192], P('head', 'dp'), may hold values from -0.09375 to 0.09375
- grad_out: bfloat16 [2048, 8192], P(('dp', 'head')), may hold values from -6 to 6
Outputs:
- proj_out: bfloat16 [2048, 8192], P(('dp', 'head'))
- grad_attn: bfloat16 [2048, 8192], P('dp', 'head')
- grad_w: float32 [8192, 8192], P('head', 'dp')
Inputs may be any that keep to these rules, and one draw needn't show every extreme that they name: `head_mask`: exactly 32 heads are live.
All inputs are finite; a program needn't handle non-finite values.
Results may differ from a plain program's by a relative error of at most 0.0051.
Values may be sent and summed in bfloat16 or wider, within the bound.
No kernel may reach another device: no remote copies, remote signals or barrier semaphores. Data moves between devices by JAX's collectives and lax.ppermute only.
A program may use at most 128 MiB of HBM per device.

v0:
```python
import jax
import jax.numpy as jnp
from jax import lax
from jax.sharding import Mesh, PartitionSpec as P

BF = jnp.bfloat16
F32 = jnp.float32
XC = ("x", "c")


def exchange(v, axes):
    return lax.all_to_all(v, axes, split_axis=0, concat_axis=0, tiled=False)


def shift(v, axis, s):
    n = lax.axis_size(axis)
    return lax.ppermute(v, axis, [(i, (i + s) % n) for i in range(n)])


def relative(v):
    nx = v.shape[0]
    ring = jnp.concatenate([v[::-1], v[::-1]])
    v = lax.dynamic_slice_in_dim(ring, nx - 1 - lax.axis_index("x"), nx, 0)
    return jnp.where(lax.axis_index("c") == 0, v, v[:, ::-1])


def shards(attn_out, head_mask, gate_scale, w_out, grad_out):
    nx, ny, nz, nc = (lax.axis_size(a) for a in "xyzc")
    me = lax.axis_index("y")
    t, r = attn_out.shape
    j, d = grad_out.shape
    n = d // (nx * nc)
    ty = t // ny
    half = r // 2
    g = exchange(grad_out.reshape(j, nx * nc, n).transpose(1, 0, 2), XC)
    g = relative(g.reshape(nx, nc, j, n)).transpose(1, 0, 2, 3)
    gate_vals = head_mask.astype(F32) * gate_scale
    col_gate = jnp.repeat(gate_vals, r // gate_vals.shape[0])
    gated = (attn_out.astype(F32) * col_gate[None, :]).astype(BF).reshape(ny, ty, r)
    a = [lax.dynamic_index_in_dim(gated, (me + s) % ny, 0, keepdims=False) for s in range(ny)]
    a = [a[0]] + [shift(a[s], "y", s) for s in range(1, ny)]
    a = jnp.concatenate(a, axis=1)
    a, g = lax.optimization_barrier((a, g.reshape(nc * nx * j, n)))
    g = lax.all_gather(g, "z", axis=0, tiled=True)
    a = jnp.stack([a] + [shift(a, "x", s) for s in range(1, nx)])
    a = jnp.stack([a, shift(a, "c", 1)])
    w1, w3 = (shift(w_out, "y", 1), shift(w_out, "y", -1))
    w2 = [shift(w1[:half], "y", 1), shift(w3[half:], "y", -1)]
    a, w = lax.optimization_barrier((a, [w_out, w1, *w2, w3]))
    w = jnp.concatenate(w, axis=0)
    a = a.reshape(nc * nx, nz, j, ny * r).transpose(1, 0, 2, 3).reshape(nx * nc * ty, ny * r)
    part = jnp.dot(a, w, preferred_element_type=F32).astype(BF)
    proj = exchange(part.reshape(nz, nc, nx, j, n), "z").astype(F32).sum(axis=0).astype(BF)
    proj = relative(proj.transpose(1, 0, 2, 3)).reshape(nx * nc, j, n)
    proj = exchange(proj, XC)
    proj_out = proj.transpose(1, 0, 2).reshape(j, d)
    back = lax.dot_general(g, w, (((1,), (1,)), ((), ())), preferred_element_type=F32)
    back = back.reshape(nz, nc, nx, j, ny * r).transpose(1, 2, 0, 3, 4)
    own = back[0] + shift(back[1].astype(BF), "c", 1).astype(F32)
    mine = own[0]
    for s in range(1, nx):
        mine = mine + shift(own[s].astype(BF), "x", -s).astype(F32)
    mine = mine.reshape(ty, ny * r)
    mine = [mine[:, s * r : (s + 1) * r] for s in range(ny)]
    mine = [mine[0]] + [shift(mine[s], "y", -s) for s in range(1, ny)]
    ring = jnp.stack(mine + mine[:-1])
    mine = lax.dynamic_slice_in_dim(ring, (ny - me) % ny, ny, 0).reshape(t, r)
    grad_attn = (mine * col_gate[None, :]).astype(BF)
    back, g = lax.optimization_barrier((back, g))
    gw = lax.dot_general(a, g, (((0,), (0,)), ((), ())), preferred_element_type=F32)
    gw = gw.reshape(ny, 2, half, n)
    near = gw[1].at[0].add(shift(gw[2, 0].astype(BF), "y", -1).astype(F32))
    far = gw[3].at[1].add(shift(gw[2, 1].astype(BF), "y", 1).astype(F32))
    near, far = (shift(near.astype(BF), "y", -1), shift(far.astype(BF), "y", 1))
    grad_w = (gw[0] + near.astype(F32) + far.astype(F32)).reshape(r, n)
    return (proj_out, grad_attn, grad_w)


def solution(mesh):
    fine = Mesh(mesh.devices.reshape(4, 8, 4, 2), ("y", "z", "x", "c"))
    dp, head = (XC, ("y", "z"))
    return jax.shard_map(
        shards,
        mesh=fine,
        in_specs=(P(dp, head), P(head), P(head), P(head, dp), P(dp + head, None)),
        out_specs=(P(dp + head, None), P(dp, head), P(head, dp)),
        check_vma=False,
    )
```

profile of v0, /device:TPU:4, one launch (start us, length us, event | category | flops | bytes accessed | tf_op | source)
XLA Modules:
  0.0 123.9 jit_solution(1273256435222813369)
XLA Ops:
  7.2 0.7 convert_multiply_fusion
  8.0 0.1 broadcast_bitcast_fusion
  8.0 0.9 multiply_convert_fusion
  9.0 3.1 %collective-permute-start.2 = (bf16[64,256]{1,0:T(8,128)(2,1)S(1)}, bf16[64,256]{1,0:T(8,128)(2,1)S(1)}, u32[]{:S(2)}, u32[]{:S(2)}) collective-permute-start(bf16[64,256]{1,0:T(8,128)(2,1)S(1)} %get-tuple-element.62), channel_id=1, source_target_pairs={{0,192},{64,0},{128,64},{192,128},{1,193},{65,1},{129,65},{193,129... | collective-permute-start | bytes 98312 | tf_op jit(solution)/shard_map/ppermute | solution.py:17
  12.1 0.6 collective-permute-start.1
  12.7 1.0 collective-permute-start
  13.7 4.8 %all-to-all-start = ((bf16[8,8,1024]{2,1,0:T(8,128)(2,1)}), bf16[8,8,1024]{2,1,0:T(8,128)(2,1)S(1)}, u32[]{:S(2)}, u32[]{:S(2)}) async-start(bf16[8,8,1024]{2,1,0:T(8,128)(2,1)} %bitcast.130), calls=%async_computation | async-start | bytes 262144 | tf_op jit(solution)/shard_map/all_to_all | solution.py:12
  18.5 3.4 %all-to-all-done = bf16[8,8,1024]{2,1,0:T(8,128)(2,1)S(1)} async-done(((bf16[8,8,1024]{2,1,0:T(8,128)(2,1)}), bf16[8,8,1024]{2,1,0:T(8,128)(2,1)S(1)}, u32[]{:S(2)}, u32[]{:S(2)}) %all-to-all-start) | async-done | bytes 131104 | tf_op jit(solution)/shard_map/all_to_all | solution.py:12
  22.0 0.7 reverse_select_fusion.1
  22.7 1.8 %collective-permute-start.5 = (bf16[64,1024]{1,0:T(8,128)(2,1)S(1)}, bf16[64,1024]{1,0:T(8,128)(2,1)S(1)}, u32[]{:S(2)}, u32[]{:S(2)}) collective-permute-start(bf16[64,1024]{1,0:T(8,128)(2,1)S(1)} %pad_maximum_fusion.2), channel_id=1, source_target_pairs={{0,6},{2,0},{4,2},{6,4},{1,7},{3,1},{5,3},{7,5},{8,14},{10,8},{12,... | collective-permute-start | bytes 393224 | tf_op jit(solution)/shard_map/ppermute | solution.py:17
  24.5 2.1 %collective-permute-start.4 = (bf16[64,1024]{1,0:T(8,128)(2,1)S(1)}, bf16[64,1024]{1,0:T(8,128)(2,1)S(1)}, u32[]{:S(2)}, u32[]{:S(2)}) collective-permute-start(bf16[64,1024]{1,0:T(8,128)(2,1)S(1)} %pad_maximum_fusion.2), channel_id=1, source_target_pairs={{0,4},{2,6},{4,0},{6,2},{1,5},{3,7},{5,1},{7,3},{8,12},{10,14},{12... | collective-permute-start | bytes 393224 | tf_op jit(solution)/shard_map/ppermute | solution.py:17
  26.6 1.5 %collective-permute-start.3 = (bf16[64,1024]{1,0:T(8,128)(2,1)S(1)}, bf16[64,1024]{1,0:T(8,128)(2,1)S(1)}, u32[]{:S(2)}, u32[]{:S(2)}) collective-permute-start(bf16[64,1024]{1,0:T(8,128)(2,1)S(1)} %pad_maximum_fusion.2), channel_id=1, source_target_pairs={{0,2},{2,4},{4,6},{6,0},{1,3},{3,5},{5,7},{7,1},{8,10},{10,12},{12... | collective-permute-start | bytes 393224 | tf_op jit(solution)/shard_map/ppermute | solution.py:17
  28.1 2.0 %collective-permute-start.7 = (bf16[256,1024]{1,0:T(8,128)(2,1)S(1)}, bf16[256,1024]{1,0:T(8,128)(2,1)S(1)}, u32[]{:S(2)}, u32[]{:S(2)}) collective-permute-start(bf16[256,1024]{1,0:T(8,128)(2,1)S(1)} %copy-done.1), channel_id=1, source_target_pairs={{0,64},{64,128},{128,192},{192,0},{1,65},{65,129},{129,193},{193,1... | collective-permute-start | bytes 1572872 | tf_op jit(solution)/shard_map/ppermute | solution.py:17
  30.0 1.3 %collective-permute-start.9 = (bf16[256,1024]{1,0:T(8,128)(2,1)S(1)}, bf16[256,1024]{1,0:T(8,128)(2,1)S(1)}, u32[]{:S(2)}, u32[]{:S(2)}) collective-permute-start(bf16[256,1024]{1,0:T(8,128)(2,1)S(1)} %copy-done.1), channel_id=1, source_target_pairs={{0,192},{64,0},{128,64},{192,128},{1,193},{65,1},{129,65},{193,129... | collective-permute-start | bytes 1572872 | tf_op jit(solution)/shard_map/ppermute | solution.py:17
  31.4 0.8 collective-permute-done.4
  32.2 1.4 %collective-permute-done.3 = bf16[64,1024]{1,0:T(8,128)(2,1)S(1)} collective-permute-done((bf16[64,1024]{1,0:T(8,128)(2,1)S(1)}, bf16[64,1024]{1,0:T(8,128)(2,1)S(1)}, u32[]{:S(2)}, u32[]{:S(2)}) %collective-permute-start.3) | collective-permute-done | bytes 131104 | tf_op jit(solution)/shard_map/ppermute | solution.py:17
  33.6 0.1 fusion.15
  33.7 0.1 collective-permute-start.6
  33.8 8.2 %collective-permute-done.7 = bf16[256,1024]{1,0:T(8,128)(2,1)S(1)} collective-permute-done((bf16[256,1024]{1,0:T(8,128)(2,1)S(1)}, bf16[256,1024]{1,0:T(8,128)(2,1)S(1)}, u32[]{:S(2)}, u32[]{:S(2)}) %collective-permute-start.7) | collective-permute-done | bytes 524320 | tf_op jit(solution)/shard_map/ppermute | solution.py:17
  42.0 0.7 slice.127
  42.7 0.7 collective-permute-start.8
  43.4 2.6 %collective-permute-start.10 = (bf16[128,1024]{1,0:T(8,128)(2,1)S(1)}, bf16[128,1024]{1,0:T(8,128)(2,1)S(1)}, u32[]{:S(2)}, u32[]{:S(2)}) collective-permute-start(bf16[128,1024]{1,0:T(8,128)(2,1)S(1)} %slice.128), channel_id=1, source_target_pairs={{0,192},{64,0},{128,64},{192,128},{1,193},{65,1},{129,65},{193,129... | collective-permute-start | bytes 786440 | tf_op jit(solution)/shard_map/ppermute | solution.py:17
  46.1 0.1 pad_maximum_fusion
  46.2 4.3 %collective-permute-done.8 = bf16[128,1024]{1,0:T(8,128)(2,1)S(1)} collective-permute-done((bf16[128,1024]{1,0:T(8,128)(2,1)}, bf16[128,1024]{1,0:T(8,128)(2,1)S(1)}, u32[]{:S(2)}, u32[]{:S(2)}) %collective-permute-start.8) | collective-permute-done | bytes 262176 | tf_op jit(solution)/shard_map/ppermute | solution.py:17
  50.5 0.7 copy-done.3
  51.2 0.1 copy.23
  51.4 0.7 copy-done.4
  52.2 2.2 %convolution_convert_fusion = bf16[512,1024]{1,0:T(8,128)(2,1)} fusion(bf16[512,1024]{1,0:T(8,128)(2,1)S(1)} %bitcast.112, bf16[1024,1024]{1,0:T(8,128)(2,1)S(1)} %constant_dynamic-update-slice_fusion), kind=kOutput, calls=%fused_computation | convolution fusion | flops 1074266112 | bytes 4194304 | tf_op jit(solution)/shard_map/dot_general | solution.py:52
  54.5 8.5 %all-to-all-start.1 = ((bf16[8,2,4,8,1024]{4,3,2,1,0:T(8,128)(2,1)}), bf16[8,2,4,8,1024]{4,3,2,1,0:T(8,128)(2,1)S(1)}, u32[]{:S(2)}, u32[]{:S(2)}) async-start(bf16[8,2,4,8,1024]{4,3,2,1,0:T(8,128)(2,1)} %bitcast.20), calls=%async_computation.1 | async-start | bytes 2097152 | tf_op jit(solution)/shard_map/all_to_all | solution.py:12
  63.0 8.3 %all-gather.2.cloned.1.call-done = bf16[512,1024]{1,0:T(8,128)(2,1)} async-done(((bf16[64,1024]{1,0:T(8,128)(2,1)}), bf16[512,1024]{1,0:T(8,128)(2,1)}) %all-gather.2.cloned.1.call-update) | async-done | bytes 1048592 | tf_op jit(solution)/shard_map/all_gather | solution.py:44
  71.3 3.3 %fusion.21 = f32[512,1024]{1,0:T(8,128)S(1)} fusion(bf16[512,1024]{1,0:T(8,128)(2,1)} %all-gather.2.cloned.1.call-done, bf16[1024,1024]{1,0:T(8,128)(2,1)} %copy-done.5), kind=kOutput, calls=%fused_computation.61 | convolution fusion | flops 1073741824 | bytes 5242880 | tf_op jit(solution)/shard_map/dot_general | solution.py:57
  74.6 0.1 fusion.1
  74.6 0.3 collective-permute-start.11
  74.9 1.3 %fusion.20 = (bf16[1024,1024]{1,0:T(8,128)(2,1)S(1)}, f32[1024,1024]{1,0:T(8,128)S(1)}) fusion(bf16[512,1024]{1,0:T(8,128)(2,1)S(1)} %bitcast.113, bf16[512,1024]{1,0:T(8,128)(2,1)S(1)} %copy-done), kind=kOutput, calls=%fused_computation.60 | convolution fusion | flops 1074790400 | bytes 8388608 | tf_op jit(solution)/shard_map/dot_general | solution.py:70
  76.3 2.4 %collective-permute-start.18 = (bf16[128,1024]{1,0:T(8,128)(2,1)S(1)}, bf16[128,1024]{1,0:T(8,128)(2,1)S(1)}, u32[]{:S(2)}, u32[]{:S(2)}) collective-permute-start(bf16[128,1024]{1,0:T(8,128)(2,1)S(1)} %get-tuple-element.51), channel_id=1, source_target_pairs={{0,192},{64,0},{128,64},{192,128},{1,193},{65,1},{129,65},{193,129... | collective-permute-start | bytes 786440 | tf_op jit(solution)/shard_map/ppermute | solution.py:17
  78.7 0.1 slice.139
  78.9 1.2 fusion.18
  80.0 0.2 fusion.16
  80.3 0.4 collective-permute-start.12
  80.7 1.7 %collective-permute-start.14 = (bf16[8,8,1024]{2,1,0:T(8,128)(2,1)S(1)}, bf16[8,8,1024]{2,1,0:T(8,128)(2,1)S(1)}, u32[]{:S(2)}, u32[]{:S(2)}) collective-permute-start(bf16[8,8,1024]{2,1,0:T(8,128)(2,1)S(1)} %get-tuple-element.54), channel_id=1, source_target_pairs={{0,2},{2,4},{4,6},{6,0},{1,3},{3,5},{5,7},{7,1},{8,10},{10,12},{12... | collective-permute-start | bytes 393224 | tf_op jit(solution)/shard_map/ppermute | solution.py:17
  82.4 1.0 collective-permute-start.13
  83.4 1.9 %collective-permute-done.18 = bf16[128,1024]{1,0:T(8,128)(2,1)S(1)} collective-permute-done((bf16[128,1024]{1,0:T(8,128)(2,1)S(1)}, bf16[128,1024]{1,0:T(8,128)(2,1)S(1)}, u32[]{:S(2)}, u32[]{:S(2)}) %collective-permute-start.18) | collective-permute-done | bytes 262176 | tf_op jit(solution)/shard_map/ppermute | solution.py:17
  85.3 3.0 %collective-permute-done.20 = bf16[128,1024]{1,0:T(8,128)(2,1)S(1)} collective-permute-done((bf16[128,1024]{1,0:T(8,128)(2,1)S(1)}, bf16[128,1024]{1,0:T(8,128)(2,1)S(1)}, u32[]{:S(2)}, u32[]{:S(2)}) %collective-permute-start.20) | collective-permute-done | bytes 262176 | tf_op jit(solution)/shard_map/ppermute | solution.py:17
  88.4 0.9 fusion.5
  89.3 0.4 collective-permute-start.19
  89.7 1.6 %collective-permute-start.21 = (bf16[2,128,1024]{2,1,0:T(8,128)(2,1)}, bf16[2,128,1024]{2,1,0:T(8,128)(2,1)S(1)}, u32[]{:S(2)}, u32[]{:S(2)}) collective-permute-start(bf16[2,128,1024]{2,1,0:T(8,128)(2,1)} %get-tuple-element.48), channel_id=1, source_target_pairs={{0,64},{64,128},{128,192},{192,0},{1,65},{65,129},{129,193},{193,1... | collective-permute-start | bytes 1572872 | tf_op jit(solution)/shard_map/ppermute | solution.py:17
  91.4 0.7 fusion.19
  92.1 3.1 %collective-permute-start.16 = (f32[64,256]{1,0:T(8,128)}, f32[64,256]{1,0:T(8,128)}, u32[]{:S(2)}, u32[]{:S(2)}) collective-permute-start(f32[64,256]{1,0:T(8,128)} %get-tuple-element.59), channel_id=1, source_target_pairs={{0,128},{64,192},{128,0},{192,64},{1,129},{65,193},{129,1},{193,65... | collective-permute-start | bytes 196616 | tf_op jit(solution)/shard_map/ppermute | solution.py:17
  95.2 1.0 collective-permute-start.15
  96.1 0.6 fusion.13
  96.8 0.2 reduce_sum.12
  97.1 0.7 copy.24
  97.7 6.3 %all-to-all-start.2 = ((bf16[8,8,1024]{2,1,0:T(8,128)(2,1)}), bf16[8,8,1024]{2,1,0:T(8,128)(2,1)S(1)}, u32[]{:S(2)}, u32[]{:S(2)}) async-start(bf16[8,8,1024]{2,1,0:T(8,128)(2,1)} %bitcast.22), calls=%async_computation.2 | async-start | bytes 262144 | tf_op jit(solution)/shard_map/all_to_all | solution.py:12
  104.0 1.6 %collective-permute-done.15 = f32[64,256]{1,0:T(8,128)} collective-permute-done((f32[64,256]{1,0:T(8,128)}, f32[64,256]{1,0:T(8,128)}, u32[]{:S(2)}, u32[]{:S(2)}) %collective-permute-start.15) | collective-permute-done | bytes 65568 | tf_op jit(solution)/shard_map/ppermute | solution.py:17
  105.6 1.5 %bitcast_dynamic-update-slice_fusion.3 = f32[7,64,256]{2,1,0:T(8,128)} fusion(f32[7,64,256]{2,1,0:T(8,128)} %fusion.13, f32[64,256]{1,0:T(8,128)} %collective-permute-done.15), kind=kLoop, calls=%fused_computation.40 | loop fusion | bytes 131072
  107.1 1.5 %bitcast_dynamic-update-slice_fusion.1 = f32[7,64,256]{2,1,0:T(8,128)} fusion(f32[7,64,256]{2,1,0:T(8,128)} %bitcast_dynamic-update-slice_fusion.3, f32[64,256]{1,0:T(8,128)} %collective-permute-done.16), kind=kLoop, calls=%fused_computation.38 | loop fusion | bytes 131072
  108.6 1.5 %bitcast_dynamic-update-slice_fusion = f32[7,64,256]{2,1,0:T(8,128)} fusion(f32[7,64,256]{2,1,0:T(8,128)} %bitcast_dynamic-update-slice_fusion.1, f32[64,256]{1,0:T(8,128)} %collective-permute-done.17), kind=kLoop, calls=%fused_computation.37 | loop fusion | bytes 131072
  110.0 0.6 fusion.14
  110.7 1.5 %bitcast_dynamic-update-slice_fusion.4 = f32[7,64,256]{2,1,0:T(8,128)} fusion(f32[7,64,256]{2,1,0:T(8,128)} %fusion.14, f32[64,256]{1,0:T(8,128)} %collective-permute-done.15), kind=kLoop, calls=%fused_computation.41 | loop fusion | bytes 131072
  112.1 1.5 %bitcast_dynamic-update-slice_fusion.2 = f32[7,64,256]{2,1,0:T(8,128)} fusion(f32[7,64,256]{2,1,0:T(8,128)} %bitcast_dynamic-update-slice_fusion.4, f32[64,256]{1,0:T(8,128)} %collective-permute-done.16), kind=kLoop, calls=%fused_computation.39 | loop fusion | bytes 131072 | tf_op jit(solution)/shard_map/stack | solution.py:66
  113.6 1.0 constant_dynamic-slice_fusion
  114.6 0.7 fusion.10
  115.2 1.2 convert_add_fusion
  116.4 0.7 copy.46
  (48 shorter events, 0.6 us)
Async XLA Ops:
  7.2 20.9 %copy-start.1 = (bf16[256,1024]{1,0:T(8,128)(2,1)S(1)}, bf16[256,1024]{1,0:T(8,128)(2,1)}, u32[]{:S(2)}) copy-start(bf16[256,1024]{1,0:T(8,128)(2,1)} %param.12) | copy-start | bytes 1572868
  9.0 9.5 %collective-permute-start.2 = (bf16[64,256]{1,0:T(8,128)(2,1)S(1)}, bf16[64,256]{1,0:T(8,128)(2,1)S(1)}, u32[]{:S(2)}, u32[]{:S(2)}) collective-permute-start(bf16[64,256]{1,0:T(8,128)(2,1)S(1)} %get-tuple-element.62), channel_id=1, source_target_pairs={{0,192},{64,0},{128,64},{192,128},{1,193},{65,1},{129,65},{193,129... | collective-permute-start | bytes 98312 | tf_op jit(solution)/shard_map/ppermute | solution.py:17
  12.1 6.4 %collective-permute-start.1 = (bf16[64,256]{1,0:T(8,128)(2,1)S(1)}, bf16[64,256]{1,0:T(8,128)(2,1)S(1)}, u32[]{:S(2)}, u32[]{:S(2)}) collective-permute-start(bf16[64,256]{1,0:T(8,128)(2,1)S(1)} %get-tuple-element.63), channel_id=1, source_target_pairs={{0,128},{64,192},{128,0},{192,64},{1,129},{65,193},{129,1},{193,65... | collective-permute-start | bytes 98312 | tf_op jit(solution)/shard_map/ppermute | solution.py:17
  12.7 5.8 %collective-permute-start = (bf16[64,256]{1,0:T(8,128)(2,1)S(1)}, bf16[64,256]{1,0:T(8,128)(2,1)S(1)}, u32[]{:S(2)}, u32[]{:S(2)}) collective-permute-start(bf16[64,256]{1,0:T(8,128)(2,1)S(1)} %get-tuple-element.64), channel_id=1, source_target_pairs={{0,64},{64,128},{128,192},{192,0},{1,65},{65,129},{129,193},{193,1... | collective-permute-start | bytes 98312 | tf_op jit(solution)/shard_map/ppermute | solution.py:17
  13.7 8.2 %all-to-all-start = ((bf16[8,8,1024]{2,1,0:T(8,128)(2,1)}), bf16[8,8,1024]{2,1,0:T(8,128)(2,1)S(1)}, u32[]{:S(2)}, u32[]{:S(2)}) async-start(bf16[8,8,1024]{2,1,0:T(8,128)(2,1)} %bitcast.130), calls=%async_computation | async-start | bytes 262144 | tf_op jit(solution)/shard_map/all_to_all | solution.py:12
  18.5 52.8 %all-gather.2.cloned.1.call-start = ((), (), s32[]{:S(2)}) async-start(), calls=%async_computation.3 | async-start | bytes 1179648 | tf_op jit(solution)/shard_map/all_gather | solution.py:44
  22.7 8.7 %collective-permute-start.5 = (bf16[64,1024]{1,0:T(8,128)(2,1)S(1)}, bf16[64,1024]{1,0:T(8,128)(2,1)S(1)}, u32[]{:S(2)}, u32[]{:S(2)}) collective-permute-start(bf16[64,1024]{1,0:T(8,128)(2,1)S(1)} %pad_maximum_fusion.2), channel_id=1, source_target_pairs={{0,6},{2,0},{4,2},{6,4},{1,7},{3,1},{5,3},{7,5},{8,14},{10,8},{12,... | collective-permute-start | bytes 393224 | tf_op jit(solution)/shard_map/ppermute | solution.py:17
  24.5 7.7 %collective-permute-start.4 = (bf16[64,1024]{1,0:T(8,128)(2,1)S(1)}, bf16[64,1024]{1,0:T(8,128)(2,1)S(1)}, u32[]{:S(2)}, u32[]{:S(2)}) collective-permute-start(bf16[64,1024]{1,0:T(8,128)(2,1)S(1)} %pad_maximum_fusion.2), channel_id=1, source_target_pairs={{0,4},{2,6},{4,0},{6,2},{1,5},{3,7},{5,1},{7,3},{8,12},{10,14},{12... | collective-permute-start | bytes 393224 | tf_op jit(solution)/shard_map/ppermute | solution.py:17
  26.6 7.0 %collective-permute-start.3 = (bf16[64,1024]{1,0:T(8,128)(2,1)S(1)}, bf16[64,1024]{1,0:T(8,128)(2,1)S(1)}, u32[]{:S(2)}, u32[]{:S(2)}) collective-permute-start(bf16[64,1024]{1,0:T(8,128)(2,1)S(1)} %pad_maximum_fusion.2), channel_id=1, source_target_pairs={{0,2},{2,4},{4,6},{6,0},{1,3},{3,5},{5,7},{7,1},{8,10},{10,12},{12... | collective-permute-start | bytes 393224 | tf_op jit(solution)/shard_map/ppermute | solution.py:17
  28.1 13.9 %collective-permute-start.7 = (bf16[256,1024]{1,0:T(8,128)(2,1)S(1)}, bf16[256,1024]{1,0:T(8,128)(2,1)S(1)}, u32[]{:S(2)}, u32[]{:S(2)}) collective-permute-start(bf16[256,1024]{1,0:T(8,128)(2,1)S(1)} %copy-done.1), channel_id=1, source_target_pairs={{0,64},{64,128},{128,192},{192,0},{1,65},{65,129},{129,193},{193,1... | collective-permute-start | bytes 1572872 | tf_op jit(solution)/shard_map/ppermute | solution.py:17
  30.0 13.4 %collective-permute-start.9 = (bf16[256,1024]{1,0:T(8,128)(2,1)S(1)}, bf16[256,1024]{1,0:T(8,128)(2,1)S(1)}, u32[]{:S(2)}, u32[]{:S(2)}) collective-permute-start(bf16[256,1024]{1,0:T(8,128)(2,1)S(1)} %copy-done.1), channel_id=1, source_target_pairs={{0,192},{64,0},{128,64},{192,128},{1,193},{65,1},{129,65},{193,129... | collective-permute-start | bytes 1572872 | tf_op jit(solution)/shard_map/ppermute | solution.py:17
  33.7 12.4 %collective-permute-start.6 = (bf16[4,64,1024]{2,1,0:T(8,128)(2,1)S(1)}, bf16[4,64,1024]{2,1,0:T(8,128)(2,1)S(1)}, u32[]{:S(2)}, u32[]{:S(2)}) collective-permute-start(bf16[4,64,1024]{2,1,0:T(8,128)(2,1)S(1)} %get-tuple-element.57), channel_id=1, source_target_pairs={{0,1},{1,0},{2,3},{3,2},{4,5},{5,4},{6,7},{7,6},{8,9},{9,8},{10,11... | collective-permute-start | bytes 1572872 | tf_op jit(solution)/shard_map/ppermute | solution.py:17
  42.7 7.8 %collective-permute-start.8 = (bf16[128,1024]{1,0:T(8,128)(2,1)}, bf16[128,1024]{1,0:T(8,128)(2,1)S(1)}, u32[]{:S(2)}, u32[]{:S(2)}) collective-permute-start(bf16[128,1024]{1,0:T(8,128)(2,1)} %slice.127), channel_id=1, source_target_pairs={{0,64},{64,128},{128,192},{192,0},{1,65},{65,129},{129,193},{193,1... | collective-permute-start | bytes 786440 | tf_op jit(solution)/shard_map/ppermute | solution.py:17
  43.4 7.1 %collective-permute-start.10 = (bf16[128,1024]{1,0:T(8,128)(2,1)S(1)}, bf16[128,1024]{1,0:T(8,128)(2,1)S(1)}, u32[]{:S(2)}, u32[]{:S(2)}) collective-permute-start(bf16[128,1024]{1,0:T(8,128)(2,1)S(1)} %slice.128), channel_id=1, source_target_pairs={{0,192},{64,0},{128,64},{192,128},{1,193},{65,1},{129,65},{193,129... | collective-permute-start | bytes 786440 | tf_op jit(solution)/shard_map/ppermute | solution.py:17
  46.1 5.3 %copy-start.2 = (bf16[256,1024]{1,0:T(8,128)(2,1)S(1)}, bf16[256,1024]{1,0:T(8,128)(2,1)}, u32[]{:S(2)}) copy-start(bf16[256,1024]{1,0:T(8,128)(2,1)} %param.12) | copy-start | bytes 1572868
  50.5 0.7 copy-start.3
  51.2 0.9 copy-start.4
  52.2 2.3 %copy-start.5 = (bf16[1024,1024]{1,0:T(8,128)(2,1)}, bf16[1024,1024]{1,0:T(8,128)(2,1)S(1)}, u32[]{:S(2)}) copy-start(bf16[1024,1024]{1,0:T(8,128)(2,1)S(1)} %constant_dynamic-update-slice_fusion) | copy-start | bytes 6291460
  54.5 42.3 %all-to-all-start.1 = ((bf16[8,2,4,8,1024]{4,3,2,1,0:T(8,128)(2,1)}), bf16[8,2,4,8,1024]{4,3,2,1,0:T(8,128)(2,1)S(1)}, u32[]{:S(2)}, u32[]{:S(2)}) async-start(bf16[8,2,4,8,1024]{4,3,2,1,0:T(8,128)(2,1)} %bitcast.20), calls=%async_computation.1 | async-start | bytes 2097152 | tf_op jit(solution)/shard_map/all_to_all | solution.py:12
  71.3 3.6 %copy-start = (bf16[512,1024]{1,0:T(8,128)(2,1)S(1)}, bf16[512,1024]{1,0:T(8,128)(2,1)}, u32[]{:S(2)}) copy-start(bf16[512,1024]{1,0:T(8,128)(2,1)} %all-gather.2.cloned.1.call-done) | copy-start | bytes 3145732
  74.6 5.4 %collective-permute-start.11 = (bf16[4,8,8,1024]{3,2,0,1:T(8,128)(2,1)S(1)}, bf16[4,8,8,1024]{3,2,0,1:T(8,128)(2,1)S(1)}, u32[]{:S(2)}, u32[]{:S(2)}) collective-permute-start(bf16[4,8,8,1024]{3,2,0,1:T(8,128)(2,1)S(1)} %fusion.1), channel_id=1, source_target_pairs={{0,1},{1,0},{2,3},{3,2},{4,5},{5,4},{6,7},{7,6},{8,9},{9,8},{10,11... | collective-permute-start | bytes 1572872 | tf_op jit(solution)/shard_map/ppermute | solution.py:17
  76.3 9.0 %collective-permute-start.18 = (bf16[128,1024]{1,0:T(8,128)(2,1)S(1)}, bf16[128,1024]{1,0:T(8,128)(2,1)S(1)}, u32[]{:S(2)}, u32[]{:S(2)}) collective-permute-start(bf16[128,1024]{1,0:T(8,128)(2,1)S(1)} %get-tuple-element.51), channel_id=1, source_target_pairs={{0,192},{64,0},{128,64},{192,128},{1,193},{65,1},{129,65},{193,129... | collective-permute-start | bytes 786440 | tf_op jit(solution)/shard_map/ppermute | solution.py:17
  78.7 9.6 %collective-permute-start.20 = (bf16[128,1024]{1,0:T(8,128)(2,1)S(1)}, bf16[128,1024]{1,0:T(8,128)(2,1)S(1)}, u32[]{:S(2)}, u32[]{:S(2)}) collective-permute-start(bf16[128,1024]{1,0:T(8,128)(2,1)S(1)} %get-tuple-element.52), channel_id=1, source_target_pairs={{0,64},{64,128},{128,192},{192,0},{1,65},{65,129},{129,193},{193,1... | collective-permute-start | bytes 786440 | tf_op jit(solution)/shard_map/ppermute | solution.py:17
  80.3 11.1 %collective-permute-start.12 = (bf16[8,8,1024]{2,1,0:T(8,128)(2,1)S(1)}, bf16[8,8,1024]{2,1,0:T(8,128)(2,1)S(1)}, u32[]{:S(2)}, u32[]{:S(2)}) collective-permute-start(bf16[8,8,1024]{2,1,0:T(8,128)(2,1)S(1)} %get-tuple-element.53), channel_id=1, source_target_pairs={{0,6},{2,0},{4,2},{6,4},{1,7},{3,1},{5,3},{7,5},{8,14},{10,8},{12,... | collective-permute-start | bytes 393224 | tf_op jit(solution)/shard_map/ppermute | solution.py:17
  80.7 10.7 %collective-permute-start.14 = (bf16[8,8,1024]{2,1,0:T(8,128)(2,1)S(1)}, bf16[8,8,1024]{2,1,0:T(8,128)(2,1)S(1)}, u32[]{:S(2)}, u32[]{:S(2)}) collective-permute-start(bf16[8,8,1024]{2,1,0:T(8,128)(2,1)S(1)} %get-tuple-element.54), channel_id=1, source_target_pairs={{0,2},{2,4},{4,6},{6,0},{1,3},{3,5},{5,7},{7,1},{8,10},{10,12},{12... | collective-permute-start | bytes 393224 | tf_op jit(solution)/shard_map/ppermute | solution.py:17
  82.4 9.0 %collective-permute-start.13 = (bf16[8,8,1024]{2,1,0:T(8,128)(2,1)S(1)}, bf16[8,8,1024]{2,1,0:T(8,128)(2,1)S(1)}, u32[]{:S(2)}, u32[]{:S(2)}) collective-permute-start(bf16[8,8,1024]{2,1,0:T(8,128)(2,1)S(1)} %get-tuple-element.55), channel_id=1, source_target_pairs={{0,4},{2,6},{4,0},{6,2},{1,5},{3,7},{5,1},{7,3},{8,12},{10,14},{12... | collective-permute-start | bytes 393224 | tf_op jit(solution)/shard_map/ppermute | solution.py:17
  89.3 25.9 %collective-permute-start.19 = (bf16[2,128,1024]{2,1,0:T(8,128)(2,1)}, bf16[2,128,1024]{2,1,0:T(8,128)(2,1)S(1)}, u32[]{:S(2)}, u32[]{:S(2)}) collective-permute-start(bf16[2,128,1024]{2,1,0:T(8,128)(2,1)} %get-tuple-element.47), channel_id=1, source_target_pairs={{0,192},{64,0},{128,64},{192,128},{1,193},{65,1},{129,65},{193,129... | collective-permute-start | bytes 1572872 | tf_op jit(solution)/shard_map/ppermute | solution.py:17
  89.7 25.5 %collective-permute-start.21 = (bf16[2,128,1024]{2,1,0:T(8,128)(2,1)}, bf16[2,128,1024]{2,1,0:T(8,128)(2,1)S(1)}, u32[]{:S(2)}, u32[]{:S(2)}) collective-permute-start(bf16[2,128,1024]{2,1,0:T(8,128)(2,1)} %get-tuple-element.48), channel_id=1, source_target_pairs={{0,64},{64,128},{128,192},{192,0},{1,65},{65,129},{129,193},{193,1... | collective-permute-start | bytes 1572872 | tf_op jit(solution)/shard_map/ppermute | solution.py:17
  92.1 16.5 %collective-permute-start.17 = (f32[64,256]{1,0:T(8,128)}, f32[64,256]{1,0:T(8,128)}, u32[]{:S(2)}, u32[]{:S(2)}) collective-permute-start(f32[64,256]{1,0:T(8,128)} %get-tuple-element.58), channel_id=1, source_target_pairs={{0,64},{64,128},{128,192},{192,0},{1,65},{65,129},{129,193},{193,1... | collective-permute-start | bytes 196616 | tf_op jit(solution)/shard_map/ppermute | solution.py:17
  92.1 15.0 %collective-permute-start.16 = (f32[64,256]{1,0:T(8,128)}, f32[64,256]{1,0:T(8,128)}, u32[]{:S(2)}, u32[]{:S(2)}) collective-permute-start(f32[64,256]{1,0:T(8,128)} %get-tuple-element.59), channel_id=1, source_target_pairs={{0,128},{64,192},{128,0},{192,64},{1,129},{65,193},{129,1},{193,65... | collective-permute-start | bytes 196616 | tf_op jit(solution)/shard_map/ppermute | solution.py:17
  95.2 10.5 %collective-permute-start.15 = (f32[64,256]{1,0:T(8,128)}, f32[64,256]{1,0:T(8,128)}, u32[]{:S(2)}, u32[]{:S(2)}) collective-permute-start(f32[64,256]{1,0:T(8,128)} %get-tuple-element.60), channel_id=1, source_target_pairs={{0,192},{64,0},{128,64},{192,128},{1,193},{65,1},{129,65},{193,129... | collective-permute-start | bytes 196616 | tf_op jit(solution)/shard_map/ppermute | solution.py:17
  97.7 17.5 %all-to-all-start.2 = ((bf16[8,8,1024]{2,1,0:T(8,128)(2,1)}), bf16[8,8,1024]{2,1,0:T(8,128)(2,1)S(1)}, u32[]{:S(2)}, u32[]{:S(2)}) async-start(bf16[8,8,1024]{2,1,0:T(8,128)(2,1)} %bitcast.22), calls=%async_computation.2 | async-start | bytes 262144 | tf_op jit(solution)/shard_map/all_to_all | solution.py:12
Sparse Core Ops, SparseCore 0:
  28.2 43.0 all-gather.1
where the time goes:
time: 125 us; the launch traced here: 124 us
  starting transfers between devices  48.2 us (39%)
  waiting for transfers between devices  33.1 us (26%)
  local copies, waits for them, and re-layouts  15.4 us (12%)
  between operations  14.4 us (12%)
  matrix products  6.85 us (5%)
  other arithmetic  5.94 us (5%)
    ppermute x22, starting transfers between devices, shift(): return lax.ppermute(v, axis, [(i, (i + s) % n) for i in range(n)])  28.7 us
    ppermute x22, waiting for transfers between devices, shift(): return lax.ppermute(v, axis, [(i, (i + s) % n) for i in range(n)])  21.4 us
    all_to_all x3, starting transfers between devices, exchange(): return lax.all_to_all(v, axes, split_axis=0, concat_axis=0, tiled=False)  19.5 us
    unnamed x23, local copies, waits for them, and re-layouts  9.32 us
    all_gather x1, waiting for transfers between devices, shards(): g = lax.all_gather(g, 'z', axis=0, tiled=True)  8.31 us
    all_to_all x3, waiting for transfers between devices, exchange(): return lax.all_to_all(v, axes, split_axis=0, concat_axis=0, tiled=False)  3.38 us
    dot_general x1, matrix products, shards(): lax.dot_general(g, w, (((1,), (1,)), ((), ())), preferred_element_type=F32)  3.28 us
  transfers between devices with their start and end apart: 26, of which 9 were waited for; matrix products, arithmetic and copies ran while one was open for 18% of the time, Pallas kernels for 0%

commit v1 on v0

--- a/solution.py
+++ b/solution.py
@@ -41,7 +41,15 @@
     a = [a[0]] + [shift(a[s], "y", s) for s in range(1, ny)]
     a = jnp.concatenate(a, axis=1)
     a, g = lax.optimization_barrier((a, g.reshape(nc * nx * j, n)))
-    g = lax.all_gather(g, "z", axis=0, tiled=True)
+    g = jnp.concatenate(
+        jax.lax.all_to_all(
+            jnp.stack([g for _ in range(jax.lax.axis_size("z"))]),
+            concat_axis=0,
+            axis_name="z",
+            split_axis=0,
+        ),
+        axis=0,
+    )
     a = jnp.stack([a] + [shift(a, "x", s) for s in range(1, nx)])
     a = jnp.stack([a, shift(a, "c", 1)])
     w1, w3 = (shift(w_out, "y", 1), shift(w_out, "y", -1))

time: 125 us -> 114 us (0.912)
  between operations: 14.4 us -> 0.95 us
  waiting for transfers between devices: 33.1 us -> 22.8 us
  starting transfers between devices: 48.2 us -> 55.5 us
  local copies, waits for them, and re-layouts: 15.4 us -> 19.9 us
  other arithmetic: 5.94 us -> 7.19 us
    all_to_all x0 -> x1, starting transfers between devices: none -> 8.47 us  [shards(): jax.lax.all_to_all(jnp.stack([g for _ in range(jax.lax.axis_size('z'))]),...]
    all_gather x1 -> x0, waiting for transfers between devices: 8.31 us -> none  [shards(): g = lax.all_gather(g, 'z', axis=0, tiled=True)]
    unnamed x23 -> x15, local copies, waits for them, and re-layouts: 9.32 us -> 11.9 us
    ppermute x22, waiting for transfers between devices: 21.4 us -> 19.4 us  [shift(): return lax.ppermute(v, axis, [(i, (i + s) % n) for i in range(n)])]
    another operation x2, other arithmetic: 0.18 us -> 2.13 us  [shards(): a = jnp.stack([a, shift(a, 'c', 1)])]
    all_to_all x3, starting transfers between devices: 19.5 us -> 17.7 us  [exchange(): return lax.all_to_all(v, axes, split_axis=0, concat_axis=0, tiled=False)]
  transfers between devices with their start and end apart: 26 -> 26, of which waited for: 9 -> 7; matrix products, arithmetic and copies ran while one was open for 18% -> 25% of each run, Pallas kernels for 0% -> 0%
where the time goes in v1:
time: 114 us; the launch traced here: 113 us
  starting transfers between devices  55.5 us (49%)
  waiting for transfers between devices  22.8 us (20%)
  local copies, waits for them, and re-layouts  19.9 us (17%)
  other arithmetic  7.19 us (6%)
  matrix products  6.41 us (6%)
    ppermute x22, starting transfers between devices, shift(): return lax.ppermute(v, axis, [(i, (i + s) % n) for i in range(n)])  29.3 us
    ppermute x22, waiting for transfers between devices, shift(): return lax.ppermute(v, axis, [(i, (i + s) % n) for i in range(n)])  19.4 us
    all_to_all x3, starting transfers between devices, exchange(): return lax.all_to_all(v, axes, split_axis=0, concat_axis=0, tiled=False)  17.7 us
    unnamed x15, local copies, waits for them, and re-layouts  11.9 us
    all_to_all x1, starting transfers between devices, shards(): jax.lax.all_to_all(jnp.stack([g for _ in range(jax.lax.axis_size('z'))]),...  8.47 us
    all_to_all x3, waiting for transfers between devices, exchange(): return lax.all_to_all(v, axes, split_axis=0, concat_axis=0, tiled=False)  3.39 us
    dot_general x1, matrix products, shards(): lax.dot_general(g, w, (((1,), (1,)), ((), ())), preferred_element_type=F32)  2.87 us
  transfers between devices with their start and end apart: 26, of which 7 were waited for; matrix products, arithmetic and copies ran while one was open for 25% of the time, Pallas kernels for 0%

profile of v1, /device:TPU:4, one launch (start us, length us, event | category | flops | bytes accessed | tf_op | source)
XLA Modules:
  0.0 112.7 jit_solution(15040831009170446025)
XLA Ops:
  0.7 0.7 convert_multiply_fusion
  1.4 0.9 multiply_convert_fusion
  2.4 3.1 %collective-permute-start.2 = (bf16[64,256]{1,0:T(8,128)(2,1)S(1)}, bf16[64,256]{1,0:T(8,128)(2,1)S(1)}, u32[]{:S(2)}, u32[]{:S(2)}) collective-permute-start(bf16[64,256]{1,0:T(8,128)(2,1)S(1)} %get-tuple-element.62), channel_id=1, source_target_pairs={{0,192},{64,0},{128,64},{192,128},{1,193},{65,1},{129,65},{193,129... | collective-permute-start | bytes 98312 | tf_op jit(solution)/shard_map/ppermute | solution.py:17
  5.5 0.6 collective-permute-start.1
  6.1 1.0 collective-permute-start
  7.1 4.8 %all-to-all-start = ((bf16[8,8,1024]{2,1,0:T(8,128)(2,1)}), bf16[8,8,1024]{2,1,0:T(8,128)(2,1)S(1)}, u32[]{:S(2)}, u32[]{:S(2)}) async-start(bf16[8,8,1024]{2,1,0:T(8,128)(2,1)} %bitcast.137), calls=%async_computation | async-start | bytes 262144 | tf_op jit(solution)/shard_map/all_to_all | solution.py:12
  11.9 3.4 %all-to-all-done = bf16[8,8,1024]{2,1,0:T(8,128)(2,1)S(1)} async-done(((bf16[8,8,1024]{2,1,0:T(8,128)(2,1)}), bf16[8,8,1024]{2,1,0:T(8,128)(2,1)S(1)}, u32[]{:S(2)}, u32[]{:S(2)}) %all-to-all-start) | async-done | bytes 131104 | tf_op jit(solution)/shard_map/all_to_all | solution.py:12
  15.5 1.9 %collective-permute-start.5 = (bf16[64,1024]{1,0:T(8,128)(2,1)S(1)}, bf16[64,1024]{1,0:T(8,128)(2,1)S(1)}, u32[]{:S(2)}, u32[]{:S(2)}) collective-permute-start(bf16[64,1024]{1,0:T(8,128)(2,1)S(1)} %pad_maximum_fusion.2), channel_id=1, source_target_pairs={{0,6},{2,0},{4,2},{6,4},{1,7},{3,1},{5,3},{7,5},{8,14},{10,8},{12,... | collective-permute-start | bytes 393224 | tf_op jit(solution)/shard_map/ppermute | solution.py:17
  17.4 2.1 %collective-permute-start.4 = (bf16[64,1024]{1,0:T(8,128)(2,1)S(1)}, bf16[64,1024]{1,0:T(8,128)(2,1)S(1)}, u32[]{:S(2)}, u32[]{:S(2)}) collective-permute-start(bf16[64,1024]{1,0:T(8,128)(2,1)S(1)} %pad_maximum_fusion.2), channel_id=1, source_target_pairs={{0,4},{2,6},{4,0},{6,2},{1,5},{3,7},{5,1},{7,3},{8,12},{10,14},{12... | collective-permute-start | bytes 393224 | tf_op jit(solution)/shard_map/ppermute | solution.py:17
  19.4 1.5 %collective-permute-start.3 = (bf16[64,1024]{1,0:T(8,128)(2,1)S(1)}, bf16[64,1024]{1,0:T(8,128)(2,1)S(1)}, u32[]{:S(2)}, u32[]{:S(2)}) collective-permute-start(bf16[64,1024]{1,0:T(8,128)(2,1)S(1)} %pad_maximum_fusion.2), channel_id=1, source_target_pairs={{0,2},{2,4},{4,6},{6,0},{1,3},{3,5},{5,7},{7,1},{8,10},{10,12},{12... | collective-permute-start | bytes 393224 | tf_op jit(solution)/shard_map/ppermute | solution.py:17
  20.9 1.1 stack.61
  22.0 8.5 %all-to-all-start.3 = ((bf16[8,64,1024]{2,1,0:T(8,128)(2,1)}), bf16[8,64,1024]{2,1,0:T(8,128)(2,1)S(1)}, u32[]{:S(2)}, u32[]{:S(2)}) async-start(bf16[8,64,1024]{2,1,0:T(8,128)(2,1)} %stack.61), calls=%async_computation.3 | async-start | bytes 2097152 | tf_op jit(solution)/shard_map/all_to_all | solution.py:45
  30.5 1.9 %collective-permute-start.7 = (bf16[256,1024]{1,0:T(8,128)(2,1)}, bf16[256,1024]{1,0:T(8,128)(2,1)S(1)}, u32[]{:S(2)}, u32[]{:S(2)}) collective-permute-start(bf16[256,1024]{1,0:T(8,128)(2,1)} %param.12), channel_id=1, source_target_pairs={{0,64},{64,128},{128,192},{192,0},{1,65},{65,129},{129,193},{193,1... | collective-permute-start | bytes 1572872 | tf_op jit(solution)/shard_map/ppermute | solution.py:17
  32.3 1.3 %collective-permute-start.9 = (bf16[256,1024]{1,0:T(8,128)(2,1)}, bf16[256,1024]{1,0:T(8,128)(2,1)S(1)}, u32[]{:S(2)}, u32[]{:S(2)}) collective-permute-start(bf16[256,1024]{1,0:T(8,128)(2,1)} %param.12), channel_id=1, source_target_pairs={{0,192},{64,0},{128,64},{192,128},{1,193},{65,1},{129,65},{193,129... | collective-permute-start | bytes 1572872 | tf_op jit(solution)/shard_map/ppermute | solution.py:17
  33.7 0.6 copy-done
  34.4 1.0 fusion.20
  35.4 0.1 collective-permute-start.6
  35.5 8.8 %collective-permute-done.7 = bf16[256,1024]{1,0:T(8,128)(2,1)S(1)} collective-permute-done((bf16[256,1024]{1,0:T(8,128)(2,1)}, bf16[256,1024]{1,0:T(8,128)(2,1)S(1)}, u32[]{:S(2)}, u32[]{:S(2)}) %collective-permute-start.7) | collective-permute-done | bytes 524320 | tf_op jit(solution)/shard_map/ppermute | solution.py:17
  44.2 0.7 slice.127
  45.0 0.7 collective-permute-start.8
  45.6 0.7 slice.128
  46.4 2.6 %collective-permute-start.10 = (bf16[128,1024]{1,0:T(8,128)(2,1)}, bf16[128,1024]{1,0:T(8,128)(2,1)}, u32[]{:S(2)}, u32[]{:S(2)}) collective-permute-start(bf16[128,1024]{1,0:T(8,128)(2,1)} %slice.128), channel_id=1, source_target_pairs={{0,192},{64,0},{128,64},{192,128},{1,193},{65,1},{129,65},{193,129... | collective-permute-start | bytes 786440 | tf_op jit(solution)/shard_map/ppermute | solution.py:17
  48.9 1.1 %pad_maximum_fusion = bf16[2,4,64,1024]{3,2,1,0:T(8,128)(2,1)S(1)} fusion(bf16[1,4,64,1024]{3,2,1,0:T(8,128)(2,1)} %bitcast.16, bf16[1,4,64,1024]{3,2,1,0:T(8,128)(2,1)S(1)} %get-tuple-element.56), kind=kLoop, calls=%fused_computation.7 | loop fusion | flops 524288 | bytes 2097152 | tf_op jit(solution)/shard_map/stack | solution.py:54
  50.1 2.7 %collective-permute-done.8 = bf16[128,1024]{1,0:T(8,128)(2,1)S(1)} collective-permute-done((bf16[128,1024]{1,0:T(8,128)(2,1)}, bf16[128,1024]{1,0:T(8,128)(2,1)S(1)}, u32[]{:S(2)}, u32[]{:S(2)}) %collective-permute-start.8) | collective-permute-done | bytes 262176 | tf_op jit(solution)/shard_map/ppermute | solution.py:17
  52.7 0.4 collective-permute-done.10
  53.1 0.1 copy.30
  53.2 1.1 constant_dynamic-update-slice_fusion.4
  54.4 1.0 constant_dynamic-update-slice_fusion.1
  55.4 1.4 %copy-done.1 = bf16[1024,1024]{1,0:T(8,128)(2,1)} copy-done((bf16[1024,1024]{1,0:T(8,128)(2,1)}, bf16[1024,1024]{1,0:T(8,128)(2,1)S(1)}, u32[]{:S(2)}) %copy-start.1) | copy-done | bytes 2097176
  56.8 2.3 %convolution_convert_fusion = bf16[512,1024]{1,0:T(8,128)(2,1)} fusion(bf16[512,1024]{1,0:T(8,128)(2,1)S(1)} %bitcast.119, bf16[1024,1024]{1,0:T(8,128)(2,1)S(1)} %constant_dynamic-update-slice_fusion), kind=kOutput, calls=%fused_computation.3 | convolution fusion | flops 1074266112 | bytes 4194304 | tf_op jit(solution)/shard_map/dot_general | solution.py:60
  59.0 6.9 %all-to-all-start.1 = ((bf16[8,2,4,8,1024]{4,3,2,1,0:T(8,128)(2,1)}), bf16[8,2,4,8,1024]{4,3,2,1,0:T(8,128)(2,1)S(1)}, u32[]{:S(2)}, u32[]{:S(2)}) async-start(bf16[8,2,4,8,1024]{4,3,2,1,0:T(8,128)(2,1)} %bitcast.127), calls=%async_computation.1 | async-start | bytes 2097152 | tf_op jit(solution)/shard_map/all_to_all | solution.py:12
  65.9 2.9 %fusion.2 = f32[2,4,8,8,1024]{4,3,1,0,2:T(8,128)S(1)} fusion(bf16[8,2,4,8,1024]{4,3,2,1,0:T(8,128)(2,1)S(1)} %bitcast.123, bf16[1024,1024]{1,0:T(8,128)(2,1)} %copy-done.1), kind=kOutput, calls=%fused_computation.2 | convolution fusion | flops 1073741824 | bytes 5242880 | tf_op jit(solution)/shard_map/dot_general | solution.py:65
  68.9 0.3 collective-permute-start.11
  69.2 1.3 %fusion.25 = (bf16[1024,1024]{1,0:T(8,128)(2,1)S(1)}, f32[1024,1024]{1,0:T(8,128)S(1)}) fusion(bf16[512,1024]{1,0:T(8,128)(2,1)S(1)} %bitcast.120, bf16[512,1024]{1,0:T(8,128)(2,1)S(1)} %bitcast.124), kind=kOutput, calls=%fused_computation.63 | convolution fusion | flops 1074790400 | bytes 8388608 | tf_op jit(solution)/shard_map/dot_general | solution.py:78
  70.5 3.8 %collective-permute-start.18 = (bf16[128,1024]{1,0:T(8,128)(2,1)S(1)}, bf16[128,1024]{1,0:T(8,128)(2,1)S(1)}, u32[]{:S(2)}, u32[]{:S(2)}) collective-permute-start(bf16[128,1024]{1,0:T(8,128)(2,1)S(1)} %get-tuple-element.51), channel_id=1, source_target_pairs={{0,192},{64,0},{128,64},{192,128},{1,193},{65,1},{129,65},{193,129... | collective-permute-start | bytes 786440 | tf_op jit(solution)/shard_map/ppermute | solution.py:17
  74.3 0.1 slice.139
  74.4 1.1 %fusion.23 = (bf16[256,1024]{1,0:T(8,128)(2,1)}, bf16[256,1024]{1,0:T(8,128)(2,1)}) fusion(f32[1024,1024]{1,0:T(8,128)S(1)} %get-tuple-element.66), kind=kLoop, calls=%fused_computation.61 | loop fusion | bytes 2097152 | tf_op jit(solution)/shard_map/slice | solution.py:80
  75.5 0.2 fusion.21
  75.8 0.6 collective-permute-start.12
  76.4 1.5 %collective-permute-start.14 = (bf16[8,8,1024]{2,1,0:T(8,128)(2,1)S(1)}, bf16[8,8,1024]{2,1,0:T(8,128)(2,1)S(1)}, u32[]{:S(2)}, u32[]{:S(2)}) collective-permute-start(bf16[8,8,1024]{2,1,0:T(8,128)(2,1)S(1)} %get-tuple-element.54), channel_id=1, source_target_pairs={{0,2},{2,4},{4,6},{6,0},{1,3},{3,5},{5,7},{7,1},{8,10},{10,12},{12... | collective-permute-start | bytes 393224 | tf_op jit(solution)/shard_map/ppermute | solution.py:17
  77.9 1.2 %collective-permute-start.13 = (bf16[8,8,1024]{2,1,0:T(8,128)(2,1)S(1)}, bf16[8,8,1024]{2,1,0:T(8,128)(2,1)S(1)}, u32[]{:S(2)}, u32[]{:S(2)}) collective-permute-start(bf16[8,8,1024]{2,1,0:T(8,128)(2,1)S(1)} %get-tuple-element.55), channel_id=1, source_target_pairs={{0,4},{2,6},{4,0},{6,2},{1,5},{3,7},{5,1},{7,3},{8,12},{10,14},{12... | collective-permute-start | bytes 393224 | tf_op jit(solution)/shard_map/ppermute | solution.py:17
  79.1 1.4 %collective-permute-done.18 = bf16[128,1024]{1,0:T(8,128)(2,1)S(1)} collective-permute-done((bf16[128,1024]{1,0:T(8,128)(2,1)S(1)}, bf16[128,1024]{1,0:T(8,128)(2,1)S(1)}, u32[]{:S(2)}, u32[]{:S(2)}) %collective-permute-start.18) | collective-permute-done | bytes 262176 | tf_op jit(solution)/shard_map/ppermute | solution.py:17
  80.5 3.4 %collective-permute-done.20 = bf16[128,1024]{1,0:T(8,128)(2,1)S(1)} collective-permute-done((bf16[128,1024]{1,0:T(8,128)(2,1)S(1)}, bf16[128,1024]{1,0:T(8,128)(2,1)S(1)}, u32[]{:S(2)}, u32[]{:S(2)}) %collective-permute-start.20) | collective-permute-done | bytes 262176 | tf_op jit(solution)/shard_map/ppermute | solution.py:17
  83.9 1.0 fusion.10
  84.9 0.3 collective-permute-start.19
  85.2 1.7 %collective-permute-start.21 = (bf16[2,128,1024]{2,1,0:T(8,128)(2,1)}, bf16[2,128,1024]{2,1,0:T(8,128)(2,1)S(1)}, u32[]{:S(2)}, u32[]{:S(2)}) collective-permute-start(bf16[2,128,1024]{2,1,0:T(8,128)(2,1)} %get-tuple-element.48), channel_id=1, source_target_pairs={{0,64},{64,128},{128,192},{192,0},{1,65},{65,129},{129,193},{193,1... | collective-permute-start | bytes 1572872 | tf_op jit(solution)/shard_map/ppermute | solution.py:17
  87.0 0.7 fusion.24
  87.7 3.0 %collective-permute-start.16 = (f32[64,256]{1,0:T(8,128)}, f32[64,256]{1,0:T(8,128)}, u32[]{:S(2)}, u32[]{:S(2)}) collective-permute-start(f32[64,256]{1,0:T(8,128)} %get-tuple-element.59), channel_id=1, source_target_pairs={{0,128},{64,192},{128,0},{192,64},{1,129},{65,193},{129,1},{193,65... | collective-permute-start | bytes 196616 | tf_op jit(solution)/shard_map/ppermute | solution.py:17
  90.7 0.2 collective-permute-start.15
  90.9 0.6 fusion.18
  91.5 0.2 reduce_sum.12
  91.9 0.7 copy.31
  92.5 6.0 %all-to-all-start.2 = ((bf16[8,8,1024]{2,1,0:T(8,128)(2,1)}), bf16[8,8,1024]{2,1,0:T(8,128)(2,1)S(1)}, u32[]{:S(2)}, u32[]{:S(2)}) async-start(bf16[8,8,1024]{2,1,0:T(8,128)(2,1)} %bitcast.22), calls=%async_computation.2 | async-start | bytes 262144 | tf_op jit(solution)/shard_map/all_to_all | solution.py:12
  98.5 2.7 %collective-permute-done.15 = f32[64,256]{1,0:T(8,128)} collective-permute-done((f32[64,256]{1,0:T(8,128)}, f32[64,256]{1,0:T(8,128)}, u32[]{:S(2)}, u32[]{:S(2)}) %collective-permute-start.15) | collective-permute-done | bytes 65568 | tf_op jit(solution)/shard_map/ppermute | solution.py:17
  101.2 1.5 %bitcast_dynamic-update-slice_fusion.3 = f32[7,64,256]{2,1,0:T(8,128)} fusion(f32[7,64,256]{2,1,0:T(8,128)} %fusion.18, f32[64,256]{1,0:T(8,128)} %collective-permute-done.15), kind=kLoop, calls=%fused_computation.43 | loop fusion | bytes 131072
  102.7 1.5 %bitcast_dynamic-update-slice_fusion.1 = f32[7,64,256]{2,1,0:T(8,128)} fusion(f32[7,64,256]{2,1,0:T(8,128)} %bitcast_dynamic-update-slice_fusion.3, f32[64,256]{1,0:T(8,128)} %collective-permute-done.16), kind=kLoop, calls=%fused_computation.41 | loop fusion | bytes 131072
  104.2 1.5 %bitcast_dynamic-update-slice_fusion = f32[7,64,256]{2,1,0:T(8,128)} fusion(f32[7,64,256]{2,1,0:T(8,128)} %bitcast_dynamic-update-slice_fusion.1, f32[64,256]{1,0:T(8,128)} %collective-permute-done.17), kind=kLoop, calls=%fused_computation.40 | loop fusion | bytes 131072
  105.7 0.6 fusion.19
  106.3 1.5 %bitcast_dynamic-update-slice_fusion.4 = f32[7,64,256]{2,1,0:T(8,128)} fusion(f32[7,64,256]{2,1,0:T(8,128)} %fusion.19, f32[64,256]{1,0:T(8,128)} %collective-permute-done.15), kind=kLoop, calls=%fused_computation.44 | loop fusion | bytes 131072
  107.8 1.5 %bitcast_dynamic-update-slice_fusion.2 = f32[7,64,256]{2,1,0:T(8,128)} fusion(f32[7,64,256]{2,1,0:T(8,128)} %bitcast_dynamic-update-slice_fusion.4, f32[64,256]{1,0:T(8,128)} %collective-permute-done.16), kind=kLoop, calls=%fused_computation.42 | loop fusion | bytes 131072 | tf_op jit(solution)/shard_map/stack | solution.py:74
  109.2 1.0 constant_dynamic-slice_fusion
  110.2 0.7 fusion.15
  110.9 1.2 %convert_add_fusion = f32[2,128,1024]{2,1,0:T(8,128)} fusion(bf16[2,128,1024]{2,1,0:T(8,128)(2,1)S(1)} %collective-permute-done.21, f32[2,128,1024]{2,1,0:T(8,128)S(1)} %bitcast.122, bf16[2,128,1024]{2,1,0:T(8,128)(2,1)S(1)} %collective-permute-done.19), kind=kLoop, calls=%fused_computation.8 | loop fusion | flops 1048576 | bytes 3145728 | tf_op jit(solution)/shard_map/add | solution.py:83
  112.1 0.7 copy.54
  (40 shorter events, 0.7 us)
Async XLA Ops:
  2.4 9.5 %collective-permute-start.2 = (bf16[64,256]{1,0:T(8,128)(2,1)S(1)}, bf16[64,256]{1,0:T(8,128)(2,1)S(1)}, u32[]{:S(2)}, u32[]{:S(2)}) collective-permute-start(bf16[64,256]{1,0:T(8,128)(2,1)S(1)} %get-tuple-element.62), channel_id=1, source_target_pairs={{0,192},{64,0},{128,64},{192,128},{1,193},{65,1},{129,65},{193,129... | collective-permute-start | bytes 98312 | tf_op jit(solution)/shard_map/ppermute | solution.py:17
  5.5 6.4 %collective-permute-start.1 = (bf16[64,256]{1,0:T(8,128)(2,1)S(1)}, bf16[64,256]{1,0:T(8,128)(2,1)S(1)}, u32[]{:S(2)}, u32[]{:S(2)}) collective-permute-start(bf16[64,256]{1,0:T(8,128)(2,1)S(1)} %get-tuple-element.63), channel_id=1, source_target_pairs={{0,128},{64,192},{128,0},{192,64},{1,129},{65,193},{129,1},{193,65... | collective-permute-start | bytes 98312 | tf_op jit(solution)/shard_map/ppermute | solution.py:17
  6.1 5.8 %collective-permute-start = (bf16[64,256]{1,0:T(8,128)(2,1)S(1)}, bf16[64,256]{1,0:T(8,128)(2,1)S(1)}, u32[]{:S(2)}, u32[]{:S(2)}) collective-permute-start(bf16[64,256]{1,0:T(8,128)(2,1)S(1)} %get-tuple-element.64), channel_id=1, source_target_pairs={{0,64},{64,128},{128,192},{192,0},{1,65},{65,129},{129,193},{193,1... | collective-permute-start | bytes 98312 | tf_op jit(solution)/shard_map/ppermute | solution.py:17
  7.1 8.2 %all-to-all-start = ((bf16[8,8,1024]{2,1,0:T(8,128)(2,1)}), bf16[8,8,1024]{2,1,0:T(8,128)(2,1)S(1)}, u32[]{:S(2)}, u32[]{:S(2)}) async-start(bf16[8,8,1024]{2,1,0:T(8,128)(2,1)} %bitcast.137), calls=%async_computation | async-start | bytes 262144 | tf_op jit(solution)/shard_map/all_to_all | solution.py:12
  15.5 18.2 %collective-permute-start.5 = (bf16[64,1024]{1,0:T(8,128)(2,1)S(1)}, bf16[64,1024]{1,0:T(8,128)(2,1)S(1)}, u32[]{:S(2)}, u32[]{:S(2)}) collective-permute-start(bf16[64,1024]{1,0:T(8,128)(2,1)S(1)} %pad_maximum_fusion.2), channel_id=1, source_target_pairs={{0,6},{2,0},{4,2},{6,4},{1,7},{3,1},{5,3},{7,5},{8,14},{10,8},{12,... | collective-permute-start | bytes 393224 | tf_op jit(solution)/shard_map/ppermute | solution.py:17
  17.4 16.4 %collective-permute-start.4 = (bf16[64,1024]{1,0:T(8,128)(2,1)S(1)}, bf16[64,1024]{1,0:T(8,128)(2,1)S(1)}, u32[]{:S(2)}, u32[]{:S(2)}) collective-permute-start(bf16[64,1024]{1,0:T(8,128)(2,1)S(1)} %pad_maximum_fusion.2), channel_id=1, source_target_pairs={{0,4},{2,6},{4,0},{6,2},{1,5},{3,7},{5,1},{7,3},{8,12},{10,14},{12... | collective-permute-start | bytes 393224 | tf_op jit(solution)/shard_map/ppermute | solution.py:17
  19.4 14.3 %collective-permute-start.3 = (bf16[64,1024]{1,0:T(8,128)(2,1)S(1)}, bf16[64,1024]{1,0:T(8,128)(2,1)S(1)}, u32[]{:S(2)}, u32[]{:S(2)}) collective-permute-start(bf16[64,1024]{1,0:T(8,128)(2,1)S(1)} %pad_maximum_fusion.2), channel_id=1, source_target_pairs={{0,2},{2,4},{4,6},{6,0},{1,3},{3,5},{5,7},{7,1},{8,10},{10,12},{12... | collective-permute-start | bytes 393224 | tf_op jit(solution)/shard_map/ppermute | solution.py:17
  22.0 37.0 %all-to-all-start.3 = ((bf16[8,64,1024]{2,1,0:T(8,128)(2,1)}), bf16[8,64,1024]{2,1,0:T(8,128)(2,1)S(1)}, u32[]{:S(2)}, u32[]{:S(2)}) async-start(bf16[8,64,1024]{2,1,0:T(8,128)(2,1)} %stack.61), calls=%async_computation.3 | async-start | bytes 2097152 | tf_op jit(solution)/shard_map/all_to_all | solution.py:45
  30.5 13.8 %collective-permute-start.7 = (bf16[256,1024]{1,0:T(8,128)(2,1)}, bf16[256,1024]{1,0:T(8,128)(2,1)S(1)}, u32[]{:S(2)}, u32[]{:S(2)}) collective-permute-start(bf16[256,1024]{1,0:T(8,128)(2,1)} %param.12), channel_id=1, source_target_pairs={{0,64},{64,128},{128,192},{192,0},{1,65},{65,129},{129,193},{193,1... | collective-permute-start | bytes 1572872 | tf_op jit(solution)/shard_map/ppermute | solution.py:17
  32.3 13.3 %collective-permute-start.9 = (bf16[256,1024]{1,0:T(8,128)(2,1)}, bf16[256,1024]{1,0:T(8,128)(2,1)S(1)}, u32[]{:S(2)}, u32[]{:S(2)}) collective-permute-start(bf16[256,1024]{1,0:T(8,128)(2,1)} %param.12), channel_id=1, source_target_pairs={{0,192},{64,0},{128,64},{192,128},{1,193},{65,1},{129,65},{193,129... | collective-permute-start | bytes 1572872 | tf_op jit(solution)/shard_map/ppermute | solution.py:17
  33.7 0.7 copy-start
  35.4 13.6 %collective-permute-start.6 = (bf16[4,64,1024]{2,1,0:T(8,128)(2,1)S(1)}, bf16[4,64,1024]{2,1,0:T(8,128)(2,1)}, u32[]{:S(2)}, u32[]{:S(2)}) collective-permute-start(bf16[4,64,1024]{2,1,0:T(8,128)(2,1)S(1)} %get-tuple-element.57), channel_id=1, source_target_pairs={{0,1},{1,0},{2,3},{3,2},{4,5},{5,4},{6,7},{7,6},{8,9},{9,8},{10,11... | collective-permute-start | bytes 1572872 | tf_op jit(solution)/shard_map/ppermute | solution.py:17
  45.0 7.8 %collective-permute-start.8 = (bf16[128,1024]{1,0:T(8,128)(2,1)}, bf16[128,1024]{1,0:T(8,128)(2,1)S(1)}, u32[]{:S(2)}, u32[]{:S(2)}) collective-permute-start(bf16[128,1024]{1,0:T(8,128)(2,1)} %slice.127), channel_id=1, source_target_pairs={{0,64},{64,128},{128,192},{192,0},{1,65},{65,129},{129,193},{193,1... | collective-permute-start | bytes 786440 | tf_op jit(solution)/shard_map/ppermute | solution.py:17
  46.4 6.8 %collective-permute-start.10 = (bf16[128,1024]{1,0:T(8,128)(2,1)}, bf16[128,1024]{1,0:T(8,128)(2,1)}, u32[]{:S(2)}, u32[]{:S(2)}) collective-permute-start(bf16[128,1024]{1,0:T(8,128)(2,1)} %slice.128), channel_id=1, source_target_pairs={{0,192},{64,0},{128,64},{192,128},{1,193},{65,1},{129,65},{193,129... | collective-permute-start | bytes 786440 | tf_op jit(solution)/shard_map/ppermute | solution.py:17
  55.4 1.4 %copy-start.1 = (bf16[1024,1024]{1,0:T(8,128)(2,1)}, bf16[1024,1024]{1,0:T(8,128)(2,1)S(1)}, u32[]{:S(2)}) copy-start(bf16[1024,1024]{1,0:T(8,128)(2,1)S(1)} %constant_dynamic-update-slice_fusion) | copy-start | bytes 6291460
  59.0 32.5 %all-to-all-start.1 = ((bf16[8,2,4,8,1024]{4,3,2,1,0:T(8,128)(2,1)}), bf16[8,2,4,8,1024]{4,3,2,1,0:T(8,128)(2,1)S(1)}, u32[]{:S(2)}, u32[]{:S(2)}) async-start(bf16[8,2,4,8,1024]{4,3,2,1,0:T(8,128)(2,1)} %bitcast.127), calls=%async_computation.1 | async-start | bytes 2097152 | tf_op jit(solution)/shard_map/all_to_all | solution.py:12
  68.9 6.6 %collective-permute-start.11 = (bf16[4,8,8,1024]{3,2,0,1:T(8,128)(2,1)S(1)}, bf16[4,8,8,1024]{3,2,0,1:T(8,128)(2,1)S(1)}, u32[]{:S(2)}, u32[]{:S(2)}) collective-permute-start(bf16[4,8,8,1024]{3,2,0,1:T(8,128)(2,1)S(1)} %fusion.6), channel_id=1, source_target_pairs={{0,1},{1,0},{2,3},{3,2},{4,5},{5,4},{6,7},{7,6},{8,9},{9,8},{10,11... | collective-permute-start | bytes 1572872 | tf_op jit(solution)/shard_map/ppermute | solution.py:17
  70.5 10.0 %collective-permute-start.18 = (bf16[128,1024]{1,0:T(8,128)(2,1)S(1)}, bf16[128,1024]{1,0:T(8,128)(2,1)S(1)}, u32[]{:S(2)}, u32[]{:S(2)}) collective-permute-start(bf16[128,1024]{1,0:T(8,128)(2,1)S(1)} %get-tuple-element.51), channel_id=1, source_target_pairs={{0,192},{64,0},{128,64},{192,128},{1,193},{65,1},{129,65},{193,129... | collective-permute-start | bytes 786440 | tf_op jit(solution)/shard_map/ppermute | solution.py:17
  74.3 9.6 %collective-permute-start.20 = (bf16[128,1024]{1,0:T(8,128)(2,1)S(1)}, bf16[128,1024]{1,0:T(8,128)(2,1)S(1)}, u32[]{:S(2)}, u32[]{:S(2)}) collective-permute-start(bf16[128,1024]{1,0:T(8,128)(2,1)S(1)} %get-tuple-element.52), channel_id=1, source_target_pairs={{0,64},{64,128},{128,192},{192,0},{1,65},{65,129},{129,193},{193,1... | collective-permute-start | bytes 786440 | tf_op jit(solution)/shard_map/ppermute | solution.py:17
  75.8 11.1 %collective-permute-start.12 = (bf16[8,8,1024]{2,1,0:T(8,128)(2,1)S(1)}, bf16[8,8,1024]{2,1,0:T(8,128)(2,1)S(1)}, u32[]{:S(2)}, u32[]{:S(2)}) collective-permute-start(bf16[8,8,1024]{2,1,0:T(8,128)(2,1)S(1)} %get-tuple-element.53), channel_id=1, source_target_pairs={{0,6},{2,0},{4,2},{6,4},{1,7},{3,1},{5,3},{7,5},{8,14},{10,8},{12,... | collective-permute-start | bytes 393224 | tf_op jit(solution)/shard_map/ppermute | solution.py:17
  76.4 10.5 %collective-permute-start.14 = (bf16[8,8,1024]{2,1,0:T(8,128)(2,1)S(1)}, bf16[8,8,1024]{2,1,0:T(8,128)(2,1)S(1)}, u32[]{:S(2)}, u32[]{:S(2)}) collective-permute-start(bf16[8,8,1024]{2,1,0:T(8,128)(2,1)S(1)} %get-tuple-element.54), channel_id=1, source_target_pairs={{0,2},{2,4},{4,6},{6,0},{1,3},{3,5},{5,7},{7,1},{8,10},{10,12},{12... | collective-permute-start | bytes 393224 | tf_op jit(solution)/shard_map/ppermute | solution.py:17
  77.9 9.0 %collective-permute-start.13 = (bf16[8,8,1024]{2,1,0:T(8,128)(2,1)S(1)}, bf16[8,8,1024]{2,1,0:T(8,128)(2,1)S(1)}, u32[]{:S(2)}, u32[]{:S(2)}) collective-permute-start(bf16[8,8,1024]{2,1,0:T(8,128)(2,1)S(1)} %get-tuple-element.55), channel_id=1, source_target_pairs={{0,4},{2,6},{4,0},{6,2},{1,5},{3,7},{5,1},{7,3},{8,12},{10,14},{12... | collective-permute-start | bytes 393224 | tf_op jit(solution)/shard_map/ppermute | solution.py:17
  84.9 26.0 %collective-permute-start.19 = (bf16[2,128,1024]{2,1,0:T(8,128)(2,1)}, bf16[2,128,1024]{2,1,0:T(8,128)(2,1)S(1)}, u32[]{:S(2)}, u32[]{:S(2)}) collective-permute-start(bf16[2,128,1024]{2,1,0:T(8,128)(2,1)} %get-tuple-element.47), channel_id=1, source_target_pairs={{0,192},{64,0},{128,64},{192,128},{1,193},{65,1},{129,65},{193,129... | collective-permute-start | bytes 1572872 | tf_op jit(solution)/shard_map/ppermute | solution.py:17
  85.2 25.7 %collective-permute-start.21 = (bf16[2,128,1024]{2,1,0:T(8,128)(2,1)}, bf16[2,128,1024]{2,1,0:T(8,128)(2,1)S(1)}, u32[]{:S(2)}, u32[]{:S(2)}) collective-permute-start(bf16[2,128,1024]{2,1,0:T(8,128)(2,1)} %get-tuple-element.48), channel_id=1, source_target_pairs={{0,64},{64,128},{128,192},{192,0},{1,65},{65,129},{129,193},{193,1... | collective-permute-start | bytes 1572872 | tf_op jit(solution)/shard_map/ppermute | solution.py:17
  87.7 16.5 %collective-permute-start.17 = (f32[64,256]{1,0:T(8,128)}, f32[64,256]{1,0:T(8,128)}, u32[]{:S(2)}, u32[]{:S(2)}) collective-permute-start(f32[64,256]{1,0:T(8,128)} %get-tuple-element.58), channel_id=1, source_target_pairs={{0,64},{64,128},{128,192},{192,0},{1,65},{65,129},{129,193},{193,1... | collective-permute-start | bytes 196616 | tf_op jit(solution)/shard_map/ppermute | solution.py:17
  87.7 15.0 %collective-permute-start.16 = (f32[64,256]{1,0:T(8,128)}, f32[64,256]{1,0:T(8,128)}, u32[]{:S(2)}, u32[]{:S(2)}) collective-permute-start(f32[64,256]{1,0:T(8,128)} %get-tuple-element.59), channel_id=1, source_target_pairs={{0,128},{64,192},{128,0},{192,64},{1,129},{65,193},{129,1},{193,65... | collective-permute-start | bytes 196616 | tf_op jit(solution)/shard_map/ppermute | solution.py:17
  90.7 10.6 %collective-permute-start.15 = (f32[64,256]{1,0:T(8,128)}, f32[64,256]{1,0:T(8,128)}, u32[]{:S(2)}, u32[]{:S(2)}) collective-permute-start(f32[64,256]{1,0:T(8,128)} %get-tuple-element.60), channel_id=1, source_target_pairs={{0,192},{64,0},{128,64},{192,128},{1,193},{65,1},{129,65},{193,129... | collective-permute-start | bytes 196616 | tf_op jit(solution)/shard_map/ppermute | solution.py:17
  92.5 18.4 %all-to-all-start.2 = ((bf16[8,8,1024]{2,1,0:T(8,128)(2,1)}), bf16[8,8,1024]{2,1,0:T(8,128)(2,1)S(1)}, u32[]{:S(2)}, u32[]{:S(2)}) async-start(bf16[8,8,1024]{2,1,0:T(8,128)(2,1)} %bitcast.22), calls=%async_computation.2 | async-start | bytes 262144 | tf_op jit(solution)/shard_map/all_to_all | solution.py:12
